TPU v7x, 128 devices: a whole 4x4x4 slice. The times are simulated.
128 devices in a mesh: dp: 4 (over x), expert: 32 (over z, y, core).
Axes of the slice: x: 4, y: 4, z: 4, core: 2. Of those that a mesh axis runs over, the one named last changes fastest.
Arguments:
- tokens: bfloat16 [16384, 7168], P('expert', 'dp'), may hold values from -6 to 6
- grad_out: bfloat16 [16384, 7168], P('expert', 'dp'), may hold values from -6 to 6
- route_ids: int32 [16384, 1], P('expert'), may hold values from 0 to 31; in each aligned block of 512 rows (0 to 511, 512 to 1023, ...) at most 20 rows name the same one
- gate_codes: int32 [16384, 1], P('expert'), may hold values from 1 to 255
- gate_weight: bfloat16 [32, 7168, 1024], P('expert', 'dp'), may hold values from -0.0625 to 0.0625
- up_weight: bfloat16 [32, 7168, 1024], P('expert', 'dp'), may hold values from -0.0625 to 0.0625
- down_weight: bfloat16 [32, 1024, 7168], P('expert', None, 'dp'), may hold values from -0.1875 to 0.1875
- momentum: bfloat16 [32, 1024, 7168], P('expert', None, 'dp'), may hold values from -6 to 6
Outputs:
- grad_tokens: bfloat16 [16384, 7168], P('expert', 'dp')
- new_down: bfloat16 [32, 1024, 7168], P('expert', None, 'dp')
- new_momentum: bfloat16 [32, 1024, 7168], P('expert', None, 'dp')
Inputs may be any that keep to these rules, and one draw needn't show every extreme that they name: `route_ids`: each token names one expert. Among the 512 tokens of one index of the expert axis no expert is named by more than 20 tokens, a bound that some block reaches.
All inputs are finite; a program needn't handle non-finite values.
Results may differ from a plain program's by a relative error of at most 0.022.
Values may be sent and summed in bfloat16 or wider, within the bound.
A program may use at most 128 MiB of HBM per device.

v0:
```python
import jax
import jax.numpy as jnp
from jax import lax
from jax.sharding import PartitionSpec as P

first_beta = 0.9
second_beta = 0.9
learn_rate = 0.01
decay_rate = 3.0
soft_width = 1.0


def activate(terms):
    pre_gate = terms[:, 0, :]
    pre_up = terms[:, 1, :]
    grad_hidden = terms[:, 2, :]
    sigmoid = jax.nn.sigmoid(pre_gate)
    active = pre_gate * sigmoid
    hidden = (active * pre_up).astype(jnp.bfloat16)
    d_gate = (grad_hidden * pre_up * sigmoid * (1.0 + pre_gate * (1.0 - sigmoid))).astype(
        jnp.bfloat16
    )
    d_up = (grad_hidden * active).astype(jnp.bfloat16)
    return (hidden, d_gate, d_up)


def contract_last(left, right):
    return lax.dot_general(
        left, right, (((1,), (1,)), ((), ())), preferred_element_type=jnp.float32
    )


def contract_first(left, right):
    return lax.dot_general(
        left, right, (((0,), (0,)), ((), ())), preferred_element_type=jnp.float32
    )


def local(tokens, grad_out, route_ids, gate_codes, gate_weight, up_weight, down_weight, momentum):
    n_expert = lax.axis_size("expert")
    tok_rows, slab = tokens.shape
    top = route_ids.shape[1]
    capacity = max(2, tok_rows * top * 5 // (4 * n_expert))
    flat_ids = route_ids.reshape(-1)
    expert_iota = jnp.arange(n_expert, dtype=jnp.int32)
    onehot = (flat_ids[:, None] == expert_iota[None, :]).astype(jnp.int32)
    before = jnp.cumsum(onehot, axis=0) - onehot
    slot = jnp.sum(before * onehot, axis=1)
    target = flat_ids * capacity + slot
    slot_iota = jnp.arange(n_expert * capacity, dtype=jnp.int32)
    placed = (
        (target[None, :] == slot_iota[:, None])
        .astype(jnp.float32)
        .reshape(n_expert * capacity, tok_rows, top)
    )
    route_scale = gate_codes.astype(jnp.float32) / 256.0
    picker = jnp.sum(placed, axis=2).astype(jnp.bfloat16)
    scaler = jnp.sum(placed * route_scale[None, :, :], axis=2).astype(jnp.bfloat16)
    send_x = jnp.dot(picker, tokens, preferred_element_type=jnp.float32).astype(jnp.bfloat16)
    send_dy = jnp.dot(scaler, grad_out, preferred_element_type=jnp.float32).astype(jnp.bfloat16)
    send_x = send_x.reshape(n_expert, capacity, slab)
    send_dy = send_dy.reshape(n_expert, capacity, slab)
    recv_x, recv_dy = (
        lax.all_to_all(send_x, "expert", split_axis=0, concat_axis=0, tiled=True),
        lax.all_to_all(send_dy, "expert", split_axis=0, concat_axis=0, tiled=True),
    )
    x_rows = recv_x.reshape(-1, slab)
    dy_rows = recv_dy.reshape(-1, slab)
    w_gate = gate_weight[0]
    w_up = up_weight[0]
    w_down = down_weight[0]
    dy_part = dy_rows
    gate_part = jnp.dot(x_rows, w_gate, preferred_element_type=jnp.float32)
    up_part = jnp.dot(x_rows, w_up, preferred_element_type=jnp.float32)
    back_part = contract_last(dy_part, w_down)
    shares = lax.psum_scatter(
        jnp.stack([gate_part, up_part, back_part], axis=1).astype(jnp.bfloat16),
        "dp",
        scatter_dimension=0,
        tiled=True,
    ).astype(jnp.float32)
    hidden, d_gate, d_up = activate(shares)
    hidden_part = lax.all_gather(hidden, "dp", axis=0, tiled=True)
    gate_part = lax.all_gather(d_gate, "dp", axis=0, tiled=True)
    up_part = lax.all_gather(d_up, "dp", axis=0, tiled=True)
    dy_part = dy_rows
    grad_w = contract_first(hidden_part, dy_part)
    rows_x = contract_last(gate_part, w_gate) + contract_last(up_part, w_up)
    grad_x = rows_x
    grad_down, grad_x = (grad_w, grad_x)
    back = grad_x.astype(jnp.bfloat16).reshape(n_expert, capacity, slab)
    returned = lax.all_to_all(back, "expert", split_axis=0, concat_axis=0, tiled=True)
    returned = returned.reshape(n_expert * capacity, slab)
    grad_tokens = contract_first(picker, returned).astype(jnp.bfloat16)
    moment = momentum[0].astype(jnp.float32)
    weight = w_down.astype(jnp.float32)
    blend = first_beta * moment + (1.0 - first_beta) * grad_down
    step = blend / jnp.sqrt(blend * blend + soft_width * soft_width)
    agree = jnp.maximum(step * jnp.sign(weight), 0.0)
    new_down = (weight - learn_rate * (step + decay_rate * agree * weight)).astype(jnp.bfloat16)
    new_moment = (second_beta * moment + (1.0 - second_beta) * grad_down).astype(jnp.bfloat16)
    return (grad_tokens, new_down[None], new_moment[None])


def solution(mesh):
    placed = (
        P("expert", "dp"),
        P("expert", "dp"),
        P("expert", None),
        P("expert", None),
        P("expert", "dp", None),
        P("expert", "dp", None),
        P("expert", None, "dp"),
        P("expert", None, "dp"),
    )
    return jax.shard_map(
        local,
        mesh=mesh,
        in_specs=placed,
        out_specs=(P("expert", "dp"), P("expert", None, "dp"), P("expert", None, "dp")),
        check_vma=False,
    )
```

profile of v0, /device:TPU:0, one launch (start us, length us, event | category | flops | bytes accessed | tf_op | source)
XLA Modules:
  0.0 284.5 jit_solution(3125101756731378622)
XLA Ops:
  7.2 0.0 copy-start
  7.2 0.8 fusion.48
  8.0 1.2 reduce-window.6
  9.2 0.2 slice_reduce_fusion
  9.4 0.8 fusion.47
  10.2 0.7 multiply_add_fusion
  10.9 0.0 copy-done
  10.9 2.7 convolution_convert_fusion.1
  13.6 4.1 %reshape.132 = bf16[32,20,1792]{2,1,0:T(8,128)(2,1)} reshape(bf16[640,1792]{1,0:T(8,128)(2,1)} %convolution_convert_fusion.1) | data formatting | bytes 4587520 | tf_op jit(solution)/shard_map/reshape | solution.py:61
  17.7 8.5 %all-to-all-start = ((bf16[32,20,1792]{2,1,0:T(8,128)(2,1)}), bf16[32,20,1792]{2,1,0:T(8,128)(2,1)S(1)}, u32[]{:S(2)}, u32[]{:S(2)}) async-start(bf16[32,20,1792]{2,1,0:T(8,128)(2,1)} %reshape.132), calls=%async_computation | async-start | bytes 5505024 | tf_op jit(solution)/shard_map/all_to_all | solution.py:64
  26.3 0.0 copy-done.5
  26.3 4.3 %convolution_convert_fusion = bf16[640,1792]{1,0:T(8,128)(2,1)} fusion(bf16[512,1792]{1,0:T(8,128)(2,1)} %param.9, f32[512]{0:T(512)S(1)} %bitcast.104, s32[512]{0:T(512)S(1)} %multiply_add_fusion), kind=kOutput, calls=%fused_computation.24 | convolution fusion | flops 1176207360 | bytes 4132864 | tf_op jit(solution)/shard_map/dot_general | solution.py:60
  30.6 4.1 %reshape.134 = bf16[32,20,1792]{2,1,0:T(8,128)(2,1)} reshape(bf16[640,1792]{1,0:T(8,128)(2,1)} %convolution_convert_fusion) | data formatting | bytes 4587520 | tf_op jit(solution)/shard_map/reshape | solution.py:62
  34.7 29.1 %all-to-all-done = bf16[32,20,1792]{2,1,0:T(8,128)(2,1)S(1)} async-done(((bf16[32,20,1792]{2,1,0:T(8,128)(2,1)}), bf16[32,20,1792]{2,1,0:T(8,128)(2,1)S(1)}, u32[]{:S(2)}, u32[]{:S(2)}) %all-to-all-start) | async-done | bytes 2293792 | tf_op jit(solution)/shard_map/all_to_all | solution.py:64
  63.8 4.8 %all-to-all-start.1 = ((bf16[32,20,1792]{2,1,0:T(8,128)(2,1)}), bf16[32,20,1792]{2,1,0:T(8,128)(2,1)}, u32[]{:S(2)}, u32[]{:S(2)}) async-start(bf16[32,20,1792]{2,1,0:T(8,128)(2,1)} %reshape.134), calls=%async_computation.1 | async-start | bytes 5505024 | tf_op jit(solution)/shard_map/all_to_all | solution.py:65
  68.6 0.0 reduce-scatter.2.cloned.1.call-start
  68.6 2.1 reshape.133
  70.7 6.5 %fusion.31 = bf16[640,1,1024]{2,0,1:T(8,128)(2,1)} fusion(bf16[640,1792]{1,0:T(8,128)(2,1)} %reshape.133, bf16[1,1792,1024]{2,1,0:T(8,128)(2,1)} %param.13), kind=kOutput, calls=%fused_computation.31 | convolution fusion | flops 2349465600 | bytes 7274496 | tf_op jit(solution)/shard_map/dot_general | solution.py:74
  77.2 0.0 copy-done.2
  77.2 0.0 copy-done.6
  77.2 3.6 %fusion.34 = bf16[640,1,1024]{2,0,1:T(8,128)(2,1)} fusion(bf16[640,1792]{1,0:T(8,128)(2,1)S(1)} %copy-done.2, bf16[1,1792,1024]{2,1,0:T(8,128)(2,1)S(1)} %copy-done.6), kind=kOutput, calls=%fused_computation.32 | convolution fusion | flops 2349465600 | bytes 7274496 | tf_op jit(solution)/shard_map/dot_general | solution.py:73
  80.8 25.3 %all-to-all-done.1 = bf16[32,20,1792]{2,1,0:T(8,128)(2,1)} async-done(((bf16[32,20,1792]{2,1,0:T(8,128)(2,1)}), bf16[32,20,1792]{2,1,0:T(8,128)(2,1)}, u32[]{:S(2)}, u32[]{:S(2)}) %all-to-all-start.1) | async-done | bytes 2293792 | tf_op jit(solution)/shard_map/all_to_all | solution.py:65
  106.1 2.7 reshape.135
  108.8 0.0 copy-start.3
  108.8 0.0 copy-start.4
  108.8 4.8 %fusion.28 = bf16[640,1,1024]{2,0,1:T(8,128)(2,1)S(1)} fusion(bf16[640,1792]{1,0:T(8,128)(2,1)S(1)} %reshape.135, bf16[1,1024,1792]{2,1,0:T(8,128)(2,1)} %param.14), kind=kOutput, calls=%fused_computation.30 | convolution fusion | flops 2349465600 | bytes 7274496 | tf_op jit(solution)/shard_map/dot_general | solution.py:28
  113.6 2.1 pad_maximum_fusion
  115.7 0.0 reduce-scatter.2.cloned.1.call-update
  115.7 0.0 all-gather.6.cloned.1.call-start
  115.8 41.3 %reduce-scatter.2.cloned.1.call-done = bf16[160,3,1024]{2,0,1:T(8,128)(2,1)} async-done(((bf16[640,3,1024]{2,0,1:T(8,128)(2,1)}), bf16[160,3,1024]{2,0,1:T(8,128)(2,1)}) %reduce-scatter.2.cloned.1.call-update) | async-done | bytes 983056 | tf_op jit(solution)/shard_map/reduce_scatter | solution.py:76
  157.1 1.4 convert_element_type.104
  158.5 1.4 multiply_convert_fusion
  159.9 0.0 all-gather.6.cloned.1.call-update
  159.9 0.0 all-gather.4.cloned.1.call-start
  159.9 0.7 all-gather.4.cloned.1.call-update
  160.6 0.2 all-gather.8.cloned.1.call-start
  160.8 0.3 all-gather.8.cloned.1.call-update
  161.2 23.5 %all-gather.6.cloned.1.call-done = bf16[640,1024]{1,0:T(8,128)(2,1)} async-done(((bf16[160,1024]{1,0:T(8,128)(2,1)}), bf16[640,1024]{1,0:T(8,128)(2,1)}) %all-gather.6.cloned.1.call-update) | async-done | bytes 1310736 | tf_op jit(solution)/shard_map/all_gather | solution.py:85
  184.7 7.1 %fusion.8 = f32[640,1792]{1,0:T(8,128)} fusion(bf16[640,1024]{1,0:T(8,128)(2,1)} %all-gather.6.cloned.1.call-done, bf16[1,1792,1024]{2,1,0:T(8,128)(2,1)} %param.13), kind=kOutput, calls=%fused_computation.14 | convolution fusion | flops 2348810240 | bytes 9568256 | tf_op jit(solution)/shard_map/dot_general | solution.py:28
  191.8 20.6 %all-gather.4.cloned.1.call-done = bf16[640,1024]{1,0:T(8,128)(2,1)} async-done(((bf16[160,1024]{1,0:T(8,128)(2,1)}), bf16[640,1024]{1,0:T(8,128)(2,1)}) %all-gather.4.cloned.1.call-update) | async-done | bytes 1310736 | tf_op jit(solution)/shard_map/all_gather | solution.py:84
  212.4 7.8 %add_convert_fusion = bf16[640,1792]{1,0:T(8,128)(2,1)} fusion(f32[640,1792]{1,0:T(8,128)} %fusion.8, bf16[640,1024]{1,0:T(8,128)(2,1)} %all-gather.4.cloned.1.call-done, bf16[1,1792,1024]{2,1,0:T(8,128)(2,1)} %param.12), kind=kOutput, calls=%fused_computation.10 | convolution fusion | flops 2351104000 | bytes 11862016 | tf_op jit(solution)/shard_map/dot_general | solution.py:28
  220.2 4.1 %reshape.136 = bf16[32,20,1792]{2,1,0:T(8,128)(2,1)} reshape(bf16[640,1792]{1,0:T(8,128)(2,1)} %add_convert_fusion) | data formatting | bytes 4587520 | tf_op jit(solution)/shard_map/reshape | solution.py:91
  224.3 7.4 %all-to-all-start.2 = ((bf16[32,20,1792]{2,1,0:T(8,128)(2,1)}), bf16[32,20,1792]{2,1,0:T(8,128)(2,1)}, u32[]{:S(2)}, u32[]{:S(2)}) async-start(bf16[32,20,1792]{2,1,0:T(8,128)(2,1)} %reshape.136), calls=%async_computation.3 | async-start | bytes 5505024 | tf_op jit(solution)/shard_map/all_to_all | solution.py:92
  231.7 8.3 %all-gather.8.cloned.1.call-done = bf16[640,1024]{1,0:T(8,128)(2,1)} async-done(((bf16[160,1024]{1,0:T(8,128)(2,1)}), bf16[640,1024]{1,0:T(8,128)(2,1)}) %all-gather.8.cloned.1.call-update) | async-done | bytes 1310736 | tf_op jit(solution)/shard_map/all_gather | solution.py:83
  240.0 12.7 %convert_bitcast_fusion = (bf16[1,1024,1792]{2,1,0:T(8,128)(2,1)}, bf16[1,1024,1792]{2,1,0:T(8,128)(2,1)}) fusion(bf16[1,1024,1792]{2,1,0:T(8,128)(2,1)} %param.14, bf16[640,1024]{1,0:T(8,128)(2,1)} %all-gather.8.cloned.1.call-done, bf16[640,1792]{1,0:T(8,128)(2,1)S(1)} %reshape.135, bf16[1,1024,1792]{2,1,0:T(8,128)(2,1)} %param.15), kind=kOutput, calls=%fused_computation.22 | convolution fusion | flops 2381840384 | bytes 18284544 | tf_op jit(solution)/shard_map/dot_general | solution.py:34
  252.7 16.5 %all-to-all-done.2 = bf16[32,20,1792]{2,1,0:T(8,128)(2,1)} async-done(((bf16[32,20,1792]{2,1,0:T(8,128)(2,1)}), bf16[32,20,1792]{2,1,0:T(8,128)(2,1)}, u32[]{:S(2)}, u32[]{:S(2)}) %all-to-all-start.2) | async-done | bytes 2293792 | tf_op jit(solution)/shard_map/all_to_all | solution.py:92
  269.1 4.3 %reshape.137 = bf16[640,1792]{1,0:T(8,128)(2,1)} reshape(bf16[32,20,1792]{2,1,0:T(8,128)(2,1)} %all-to-all-done.2) | data formatting | bytes 4587520 | tf_op jit(solution)/shard_map/reshape | solution.py:93
  273.4 4.5 %convolution_convert_fusion.2 = bf16[512,1792]{1,0:T(8,128)(2,1)} fusion(bf16[640,1792]{1,0:T(8,128)(2,1)} %reshape.137, s32[512]{0:T(512)S(1)} %multiply_add_fusion), kind=kOutput, calls=%fused_computation.26 | convolution fusion | flops 1176305664 | bytes 4130816 | tf_op jit(solution)/shard_map/dot_general | solution.py:34
  (10 shorter events, 0.1 us)
Async XLA Ops:
  7.2 3.7 %copy-start = (bf16[512,1792]{1,0:T(8,128)(2,1)S(1)}, bf16[512,1792]{1,0:T(8,128)(2,1)}, u32[]{:S(2)}) copy-start(bf16[512,1792]{1,0:T(8,128)(2,1)} %param.8) | copy-start | bytes 5505028
  17.7 8.6 %copy-start.5 = (s32[512,1]{0,1:T(1,128)S(1)}, s32[512,1]{0,1:T(1,128)}, u32[]{:S(2)}) copy-start(s32[512,1]{0,1:T(1,128)} %param.11) | copy-start | bytes 6148
  17.7 46.0 %all-to-all-start = ((bf16[32,20,1792]{2,1,0:T(8,128)(2,1)}), bf16[32,20,1792]{2,1,0:T(8,128)(2,1)S(1)}, u32[]{:S(2)}, u32[]{:S(2)}) async-start(bf16[32,20,1792]{2,1,0:T(8,128)(2,1)} %reshape.132), calls=%async_computation | async-start | bytes 5505024 | tf_op jit(solution)/shard_map/all_to_all | solution.py:64
  63.8 42.3 %all-to-all-start.1 = ((bf16[32,20,1792]{2,1,0:T(8,128)(2,1)}), bf16[32,20,1792]{2,1,0:T(8,128)(2,1)}, u32[]{:S(2)}, u32[]{:S(2)}) async-start(bf16[32,20,1792]{2,1,0:T(8,128)(2,1)} %reshape.134), calls=%async_computation.1 | async-start | bytes 5505024 | tf_op jit(solution)/shard_map/all_to_all | solution.py:65
  68.6 88.5 %reduce-scatter.2.cloned.1.call-start = ((), (), s32[]{:S(2)}) async-start(), calls=%async_computation.4 | async-start | bytes 4915200 | tf_op jit(solution)/shard_map/reduce_scatter | solution.py:76
  70.7 6.5 %copy-start.2 = (bf16[640,1792]{1,0:T(8,128)(2,1)S(1)}, bf16[640,1792]{1,0:T(8,128)(2,1)}, u32[]{:S(2)}) copy-start(bf16[640,1792]{1,0:T(8,128)(2,1)} %reshape.133) | copy-start | bytes 6881284
  70.7 6.5 %copy-start.6 = (bf16[1,1792,1024]{2,1,0:T(8,128)(2,1)S(1)}, bf16[1,1792,1024]{2,1,0:T(8,128)(2,1)}, u32[]{:S(2)}) copy-start(bf16[1,1792,1024]{2,1,0:T(8,128)(2,1)} %param.12) | copy-start | bytes 11010052
  108.8 4.8 %copy-start.3 = (bf16[640,1,1024]{2,0,1:T(8,128)(2,1)S(1)}, bf16[640,1,1024]{2,0,1:T(8,128)(2,1)}, u32[]{:S(2)}) copy-start(bf16[640,1,1024]{2,0,1:T(8,128)(2,1)} %fusion.31) | copy-start | bytes 3932164
  108.8 4.8 %copy-start.4 = (bf16[640,1,1024]{2,0,1:T(8,128)(2,1)S(1)}, bf16[640,1,1024]{2,0,1:T(8,128)(2,1)}, u32[]{:S(2)}) copy-start(bf16[640,1,1024]{2,0,1:T(8,128)(2,1)} %fusion.34) | copy-start | bytes 3932164
  115.7 69.0 %all-gather.6.cloned.1.call-start = ((), (), s32[]{:S(2)}) async-start(), calls=%async_computation.6 | async-start | bytes 1638400 | tf_op jit(solution)/shard_map/all_gather | solution.py:85
  159.9 52.5 %all-gather.4.cloned.1.call-start = ((), (), s32[]{:S(2)}) async-start(), calls=%async_computation.5 | async-start | bytes 1638400 | tf_op jit(solution)/shard_map/all_gather | solution.py:84
  160.6 79.4 %all-gather.8.cloned.1.call-start = ((), (), s32[]{:S(2)}) async-start(), calls=%async_computation.7 | async-start | bytes 1638400 | tf_op jit(solution)/shard_map/all_gather | solution.py:83
  224.3 44.8 %all-to-all-start.2 = ((bf16[32,20,1792]{2,1,0:T(8,128)(2,1)}), bf16[32,20,1792]{2,1,0:T(8,128)(2,1)}, u32[]{:S(2)}, u32[]{:S(2)}) async-start(bf16[32,20,1792]{2,1,0:T(8,128)(2,1)} %reshape.136), calls=%async_computation.3 | async-start | bytes 5505024 | tf_op jit(solution)/shard_map/all_to_all | solution.py:92
  269.1 8.8 %copy-start.1 = (bf16[512,1792]{1,0:T(8,128)(2,1)S(1)}, bf16[512,1792]{1,0:T(8,128)(2,1)}, u32[]{:S(2)}) copy-start(bf16[512,1792]{1,0:T(8,128)(2,1)} %param.8) | copy-start | bytes 5505028
Sparse Core Ops, SparseCore 0:
  115.8 41.1 reduce-scatter.1
  160.0 24.6 all-gather.5
  186.9 25.4 all-gather.3
  214.5 25.4 all-gather.7
where the time goes:
time: 285 us; the launch traced here: 284 us
  waiting for transfers between devices  166 us (58%)
  matrix products  53.9 us (19%)
  local copies, waits for them, and re-layouts  21.6 us (8%)
  starting transfers between devices  21.1 us (7%)
  between operations  13.9 us (5%)
  other arithmetic  8.4 us (3%)
    reduce_scatter x1, waiting for transfers between devices, local(): lax.psum_scatter(jnp.stack([gate_part, up_part, back_part], axis=1).astyp...  41.3 us
    all_to_all x1, waiting for transfers between devices, local(): lax.all_to_all(send_x, 'expert', split_axis=0, concat_axis=0, tiled=True)  29.1 us
    all_to_all x1, waiting for transfers between devices, local(): lax.all_to_all(send_dy, 'expert', split_axis=0, concat_axis=0, tiled=True)  25.3 us
    all_gather x1, waiting for transfers between devices, local(): up_part = lax.all_gather(d_up, 'dp', axis=0, tiled=True)  23.5 us
    all_gather x1, waiting for transfers between devices, local(): gate_part = lax.all_gather(d_gate, 'dp', axis=0, tiled=True)  20.6 us
    dot_general x3, matrix products, contract_last(): lax.dot_general(left, right, (((1,), (1,)), ((), ())), preferred_element_...  19.6 us
    dot_general x2, matrix products, contract_first(): lax.dot_general(left, right, (((0,), (0,)), ((), ())), preferred_element_...  17.2 us
    all_to_all x1, waiting for transfers between devices, local(): lax.all_to_all(back, 'expert', split_axis=0, concat_axis=0, tiled=True)  16.5 us
  transfers between devices with their start and end apart: 7, of which 7 were waited for; matrix products, arithmetic and copies ran while one was open for 18% of the time, Pallas kernels for 0%

commit v1 on v0

--- a/solution.py
+++ b/solution.py
@@ -81,7 +81,24 @@
     ).astype(jnp.float32)
     hidden, d_gate, d_up = activate(shares)
     hidden_part = lax.all_gather(hidden, "dp", axis=0, tiled=True)
-    gate_part = lax.all_gather(d_gate, "dp", axis=0, tiled=True)
+    size, position, width = (lax.axis_size("dp"), lax.axis_index("dp"), d_gate.shape[0])
+    forward = [(i, (i + 1) % size) for i in range(size)]
+    backward = [(i, (i - 1) % size) for i in range(size)]
+    filled = jnp.zeros((*d_gate.shape[:0], size * width, *d_gate.shape[0 + 1 :]), d_gate.dtype)
+    filled = lax.dynamic_update_slice_in_dim(filled, d_gate, position * width, axis=0)
+    from_left = from_right = d_gate
+    middle = size // 2
+    for step_2 in range(1, middle + 1):
+        from_left = lax.ppermute(from_left, "dp", forward)
+        filled = lax.dynamic_update_slice_in_dim(
+            filled, from_left, (position - step_2) % size * width, axis=0
+        )
+        if step_2 < size - middle:
+            from_right = lax.ppermute(from_right, "dp", backward)
+            filled = lax.dynamic_update_slice_in_dim(
+                filled, from_right, (position + step_2) % size * width, axis=0
+            )
+    gate_part = filled
     up_part = lax.all_gather(d_up, "dp", axis=0, tiled=True)
     dy_part = dy_rows
     grad_w = contract_first(hidden_part, dy_part)

time: 285 us -> 264 us (0.926)
  waiting for transfers between devices: 166 us -> 147 us
  matrix products: 53.9 us -> 48.8 us
  starting transfers between devices: 21.1 us -> 24.3 us
    ppermute x0 -> x3, waiting for transfers between devices: none -> 25.7 us  [the longest x2 23.9 us: local(): from_left = lax.ppermute(from_left, 'dp', forward)]
    all_gather x1, waiting for transfers between devices: 23.5 us -> 0.93 us  [local(): up_part = lax.all_gather(d_up, 'dp', axis=0, tiled=True)]
    all_gather x1 -> x0, waiting for transfers between devices: 20.6 us -> none  [local(): gate_part = lax.all_gather(d_gate, 'dp', axis=0, tiled=True)]
    dot_general x3, matrix products: 19.6 us -> 14.5 us  [contract_last(): lax.dot_general(left, right, (((1,), (1,)), ((), ())), preferred_element_...]
    ppermute x0 -> x3, starting transfers between devices: none -> 3.24 us  [the longest x1 3 us: local(): from_right = lax.ppermute(from_right, 'dp', backward)]
  transfers between devices with their start and end apart: 7 -> 9, of which waited for: 7 -> 9; matrix products, arithmetic and copies ran while one was open for 18% -> 17% of each run, Pallas kernels for 0% -> 0%
where the time goes in v1:
time: 264 us; the launch traced here: 263 us
  waiting for transfers between devices  147 us (56%)
  matrix products  48.8 us (18%)
  starting transfers between devices  24.3 us (9%)
  local copies, waits for them, and re-layouts  20.1 us (8%)
  between operations  13.9 us (5%)
  other arithmetic  9.16 us (3%)
    reduce_scatter x1, waiting for transfers between devices, local(): lax.psum_scatter(jnp.stack([gate_part, up_part, back_part], axis=1).astyp...  41.3 us
    all_to_all x1, waiting for transfers between devices, local(): lax.all_to_all(send_x, 'expert', split_axis=0, concat_axis=0, tiled=True)  29.1 us
    all_to_all x1, waiting for transfers between devices, local(): lax.all_to_all(send_dy, 'expert', split_axis=0, concat_axis=0, tiled=True)  25.3 us
    ppermute x2, waiting for transfers between devices, local(): from_left = lax.ppermute(from_left, 'dp', forward)  23.9 us
    all_to_all x1, waiting for transfers between devices, local(): lax.all_to_all(back, 'expert', split_axis=0, concat_axis=0, tiled=True)  17.6 us
    dot_general x2, matrix products, contract_first(): lax.dot_general(left, right, (((0,), (0,)), ((), ())), preferred_element_...  17.2 us
    dot_general x3, matrix products, contract_last(): lax.dot_general(left, right, (((1,), (1,)), ((), ())), preferred_element_...  14.5 us
    all_to_all x1, starting transfers between devices, local(): lax.all_to_all(send_x, 'expert', split_axis=0, concat_axis=0, tiled=True)  8.55 us
  transfers between devices with their start and end apart: 9, of which 9 were waited for; matrix products, arithmetic and copies ran while one was open for 17% of the time, Pallas kernels for 0%

profile of v1, /device:TPU:0, one launch (start us, length us, event | category | flops | bytes accessed | tf_op | source)
XLA Modules:
  0.0 263.4 jit_solution(4205187278763887803)
XLA Ops:
  7.2 0.0 copy-start
  7.2 0.8 fusion.48
  8.0 1.2 reduce-window.6
  9.2 0.2 slice_reduce_fusion
  9.4 0.8 fusion.47
  10.2 0.7 multiply_add_fusion
  10.9 2.7 %convolution_convert_fusion.1 = bf16[640,1792]{1,0:T(8,128)(2,1)} fusion(bf16[512,1792]{1,0:T(8,128)(2,1)S(1)} %copy-done, s32[512]{0:T(512)S(1)} %multiply_add_fusion), kind=kOutput, calls=%fused_computation.25 | convolution fusion | flops 1176535040 | bytes 4130816 | tf_op jit(solution)/shard_map/dot_general | solution.py:59
  13.6 4.1 %reshape.132 = bf16[32,20,1792]{2,1,0:T(8,128)(2,1)} reshape(bf16[640,1792]{1,0:T(8,128)(2,1)} %convolution_convert_fusion.1) | data formatting | bytes 4587520 | tf_op jit(solution)/shard_map/reshape | solution.py:61
  17.7 8.5 %all-to-all-start = ((bf16[32,20,1792]{2,1,0:T(8,128)(2,1)}), bf16[32,20,1792]{2,1,0:T(8,128)(2,1)S(1)}, u32[]{:S(2)}, u32[]{:S(2)}) async-start(bf16[32,20,1792]{2,1,0:T(8,128)(2,1)} %reshape.132), calls=%async_computation | async-start | bytes 5505024 | tf_op jit(solution)/shard_map/all_to_all | solution.py:64
  26.3 4.3 %convolution_convert_fusion = bf16[640,1792]{1,0:T(8,128)(2,1)} fusion(bf16[512,1792]{1,0:T(8,128)(2,1)} %param.9, f32[512]{0:T(512)S(1)} %bitcast.107, s32[512]{0:T(512)S(1)} %multiply_add_fusion), kind=kOutput, calls=%fused_computation.24 | convolution fusion | flops 1176207360 | bytes 4132864 | tf_op jit(solution)/shard_map/dot_general | solution.py:60
  30.6 4.1 %reshape.134 = bf16[32,20,1792]{2,1,0:T(8,128)(2,1)} reshape(bf16[640,1792]{1,0:T(8,128)(2,1)} %convolution_convert_fusion) | data formatting | bytes 4587520 | tf_op jit(solution)/shard_map/reshape | solution.py:62
  34.7 29.1 %all-to-all-done = bf16[32,20,1792]{2,1,0:T(8,128)(2,1)S(1)} async-done(((bf16[32,20,1792]{2,1,0:T(8,128)(2,1)}), bf16[32,20,1792]{2,1,0:T(8,128)(2,1)S(1)}, u32[]{:S(2)}, u32[]{:S(2)}) %all-to-all-start) | async-done | bytes 2293792 | tf_op jit(solution)/shard_map/all_to_all | solution.py:64
  63.8 4.8 %all-to-all-start.1 = ((bf16[32,20,1792]{2,1,0:T(8,128)(2,1)}), bf16[32,20,1792]{2,1,0:T(8,128)(2,1)}, u32[]{:S(2)}, u32[]{:S(2)}) async-start(bf16[32,20,1792]{2,1,0:T(8,128)(2,1)} %reshape.134), calls=%async_computation.1 | async-start | bytes 5505024 | tf_op jit(solution)/shard_map/all_to_all | solution.py:65
  68.6 0.0 reduce-scatter.2.cloned.1.call-start
  68.7 2.1 reshape.133
  70.7 6.5 %fusion.31 = bf16[640,1,1024]{2,0,1:T(8,128)(2,1)} fusion(bf16[640,1792]{1,0:T(8,128)(2,1)} %reshape.133, bf16[1,1792,1024]{2,1,0:T(8,128)(2,1)} %param.13), kind=kOutput, calls=%fused_computation.31 | convolution fusion | flops 2349465600 | bytes 7274496 | tf_op jit(solution)/shard_map/dot_general | solution.py:74
  77.2 3.6 %fusion.34 = bf16[640,1,1024]{2,0,1:T(8,128)(2,1)} fusion(bf16[640,1792]{1,0:T(8,128)(2,1)S(1)} %copy-done.4, bf16[1,1792,1024]{2,1,0:T(8,128)(2,1)S(1)} %copy-done.9), kind=kOutput, calls=%fused_computation.32 | convolution fusion | flops 2349465600 | bytes 7274496 | tf_op jit(solution)/shard_map/dot_general | solution.py:73
  80.8 25.3 %all-to-all-done.1 = bf16[32,20,1792]{2,1,0:T(8,128)(2,1)} async-done(((bf16[32,20,1792]{2,1,0:T(8,128)(2,1)}), bf16[32,20,1792]{2,1,0:T(8,128)(2,1)}, u32[]{:S(2)}, u32[]{:S(2)}) %all-to-all-start.1) | async-done | bytes 2293792 | tf_op jit(solution)/shard_map/all_to_all | solution.py:65
  106.1 2.7 %reshape.135 = bf16[640,1792]{1,0:T(8,128)(2,1)S(1)} reshape(bf16[32,20,1792]{2,1,0:T(8,128)(2,1)} %all-to-all-done.1) | data formatting | bytes 4587520 | tf_op jit(solution)/shard_map/reshape | solution.py:68
  108.8 0.0 copy-start.6
  108.8 5.5 %fusion.28 = bf16[640,1,1024]{2,0,1:T(8,128)(2,1)S(1)} fusion(bf16[640,1792]{1,0:T(8,128)(2,1)S(1)} %reshape.135, bf16[1,1024,1792]{2,1,0:T(8,128)(2,1)} %param.14), kind=kOutput, calls=%fused_computation.30 | convolution fusion | flops 2349465600 | bytes 7274496 | tf_op jit(solution)/shard_map/dot_general | solution.py:28
  114.3 2.1 pad_maximum_fusion
  116.4 0.0 reduce-scatter.2.cloned.1.call-update
  116.5 0.0 all-gather.3.cloned.1.call-start
  116.5 41.3 %reduce-scatter.2.cloned.1.call-done = bf16[160,3,1024]{2,0,1:T(8,128)(2,1)} async-done(((bf16[640,3,1024]{2,0,1:T(8,128)(2,1)}), bf16[160,3,1024]{2,0,1:T(8,128)(2,1)}) %reduce-scatter.2.cloned.1.call-update) | async-done | bytes 983056 | tf_op jit(solution)/shard_map/reduce_scatter | solution.py:76
  157.8 1.4 convert_element_type.104
  159.3 1.1 multiply_convert_fusion
  160.3 0.0 all-gather.3.cloned.1.call-update
  160.4 0.0 all-gather.5.cloned.1.call-start
  160.4 0.2 broadcast_in_dim.6
  160.6 1.1 constant_dynamic-update-slice_fusion.3
  161.6 0.2 collective-permute-start
  161.9 3.0 %collective-permute-start.1 = (bf16[160,1024]{1,0:T(8,128)(2,1)}, bf16[160,1024]{1,0:T(8,128)(2,1)S(1)}, u32[]{:S(2)}, u32[]{:S(2)}) collective-permute-start(bf16[160,1024]{1,0:T(8,128)(2,1)} %get-tuple-element.4), channel_id=1, source_target_pairs={{0,96},{32,0},{64,32},{96,64},{1,97},{33,1},{65,33},{97,65},{2,98}... | collective-permute-start | bytes 983048 | tf_op jit(solution)/shard_map/ppermute | solution.py:97
  164.9 7.7 %collective-permute-done = bf16[160,1024]{1,0:T(8,128)(2,1)S(1)} collective-permute-done((bf16[160,1024]{1,0:T(8,128)(2,1)}, bf16[160,1024]{1,0:T(8,128)(2,1)S(1)}, u32[]{:S(2)}, u32[]{:S(2)}) %collective-permute-start) | collective-permute-done | bytes 327712 | tf_op jit(solution)/shard_map/ppermute | solution.py:92
  172.6 0.0 all-gather.5.cloned.1.call-update
  172.6 1.8 collective-permute-done.1
  174.5 16.2 %collective-permute-done.2 = bf16[160,1024]{1,0:T(8,128)(2,1)S(1)} collective-permute-done((bf16[160,1024]{1,0:T(8,128)(2,1)S(1)}, bf16[160,1024]{1,0:T(8,128)(2,1)S(1)}, u32[]{:S(2)}, u32[]{:S(2)}) %collective-permute-start.2) | collective-permute-done | bytes 327712 | tf_op jit(solution)/shard_map/ppermute | solution.py:92
  190.7 0.9 all-gather.3.cloned.1.call-done
  191.6 0.1 copy-done.5
  191.7 5.2 %fusion.8 = f32[640,1792]{1,0:T(8,128)S(1)} fusion(bf16[640,1024]{1,0:T(8,128)(2,1)} %all-gather.3.cloned.1.call-done, bf16[1,1792,1024]{2,1,0:T(8,128)(2,1)} %param.13), kind=kOutput, calls=%fused_computation.14 | convolution fusion | flops 2348810240 | bytes 9568256 | tf_op jit(solution)/shard_map/dot_general | solution.py:28
  196.9 3.9 %add_convert_fusion = bf16[640,1792]{1,0:T(8,128)(2,1)S(1)} fusion(f32[640,1792]{1,0:T(8,128)S(1)} %fusion.8, bf16[640,1024]{1,0:T(8,128)(2,1)} %copy-done.5, bf16[1,1792,1024]{2,1,0:T(8,128)(2,1)S(1)} %copy-done.10), kind=kOutput, calls=%fused_computation.10 | convolution fusion | flops 2351104000 | bytes 11862016 | tf_op jit(solution)/shard_map/dot_general | solution.py:28
  200.8 2.2 reshape.136
  203.1 7.5 %all-to-all-start.2 = ((bf16[32,20,1792]{2,1,0:T(8,128)(2,1)}), bf16[32,20,1792]{2,1,0:T(8,128)(2,1)}, u32[]{:S(2)}, u32[]{:S(2)}) async-start(bf16[32,20,1792]{2,1,0:T(8,128)(2,1)} %reshape.136), calls=%async_computation.3 | async-start | bytes 5505024 | tf_op jit(solution)/shard_map/all_to_all | solution.py:109
  210.6 7.2 %all-gather.5.cloned.1.call-done = bf16[640,1024]{1,0:T(8,128)(2,1)} async-done(((bf16[160,1024]{1,0:T(8,128)(2,1)}), bf16[640,1024]{1,0:T(8,128)(2,1)}) %all-gather.5.cloned.1.call-update) | async-done | bytes 1310736 | tf_op jit(solution)/shard_map/all_gather | solution.py:83
  217.8 12.7 %convert_bitcast_fusion = (bf16[1,1024,1792]{2,1,0:T(8,128)(2,1)}, bf16[1,1024,1792]{2,1,0:T(8,128)(2,1)}) fusion(bf16[1,1024,1792]{2,1,0:T(8,128)(2,1)} %param.14, bf16[640,1024]{1,0:T(8,128)(2,1)} %all-gather.5.cloned.1.call-done, bf16[640,1792]{1,0:T(8,128)(2,1)S(1)} %copy-done.3, bf16[1,1024,1792]{2,1,0:T(8,128)(2,1)} %param.15), kind=kOutput, calls=%fused_computation.22 | convolution fusion | flops 2381840384 | bytes 18284544 | tf_op jit(solution)/shard_map/dot_general | solution.py:34
  230.5 17.6 %all-to-all-done.2 = bf16[32,20,1792]{2,1,0:T(8,128)(2,1)} async-done(((bf16[32,20,1792]{2,1,0:T(8,128)(2,1)}), bf16[32,20,1792]{2,1,0:T(8,128)(2,1)}, u32[]{:S(2)}, u32[]{:S(2)}) %all-to-all-start.2) | async-done | bytes 2293792 | tf_op jit(solution)/shard_map/all_to_all | solution.py:109
  248.1 4.3 %reshape.137 = bf16[640,1792]{1,0:T(8,128)(2,1)} reshape(bf16[32,20,1792]{2,1,0:T(8,128)(2,1)} %all-to-all-done.2) | data formatting | bytes 4587520 | tf_op jit(solution)/shard_map/reshape | solution.py:110
  252.3 4.5 %convolution_convert_fusion.2 = bf16[512,1792]{1,0:T(8,128)(2,1)} fusion(bf16[640,1792]{1,0:T(8,128)(2,1)} %reshape.137, s32[512]{0:T(512)S(1)} %multiply_add_fusion), kind=kOutput, calls=%fused_computation.26 | convolution fusion | flops 1176305664 | bytes 4130816 | tf_op jit(solution)/shard_map/dot_general | solution.py:34
  (26 shorter events, 0.2 us)
Async XLA Ops:
  7.2 3.7 %copy-start = (bf16[512,1792]{1,0:T(8,128)(2,1)S(1)}, bf16[512,1792]{1,0:T(8,128)(2,1)}, u32[]{:S(2)}) copy-start(bf16[512,1792]{1,0:T(8,128)(2,1)} %param.8) | copy-start | bytes 5505028
  17.7 8.6 %copy-start.8 = (s32[512,1]{0,1:T(1,128)S(1)}, s32[512,1]{0,1:T(1,128)}, u32[]{:S(2)}) copy-start(s32[512,1]{0,1:T(1,128)} %param.11) | copy-start | bytes 6148
  17.7 46.0 %all-to-all-start = ((bf16[32,20,1792]{2,1,0:T(8,128)(2,1)}), bf16[32,20,1792]{2,1,0:T(8,128)(2,1)S(1)}, u32[]{:S(2)}, u32[]{:S(2)}) async-start(bf16[32,20,1792]{2,1,0:T(8,128)(2,1)} %reshape.132), calls=%async_computation | async-start | bytes 5505024 | tf_op jit(solution)/shard_map/all_to_all | solution.py:64
  63.8 42.3 %all-to-all-start.1 = ((bf16[32,20,1792]{2,1,0:T(8,128)(2,1)}), bf16[32,20,1792]{2,1,0:T(8,128)(2,1)}, u32[]{:S(2)}, u32[]{:S(2)}) async-start(bf16[32,20,1792]{2,1,0:T(8,128)(2,1)} %reshape.134), calls=%async_computation.1 | async-start | bytes 5505024 | tf_op jit(solution)/shard_map/all_to_all | solution.py:65
  68.6 89.2 %reduce-scatter.2.cloned.1.call-start = ((), (), s32[]{:S(2)}) async-start(), calls=%async_computation.4 | async-start | bytes 4915200 | tf_op jit(solution)/shard_map/reduce_scatter | solution.py:76
  70.7 6.5 %copy-start.4 = (bf16[640,1792]{1,0:T(8,128)(2,1)S(1)}, bf16[640,1792]{1,0:T(8,128)(2,1)}, u32[]{:S(2)}) copy-start(bf16[640,1792]{1,0:T(8,128)(2,1)} %reshape.133) | copy-start | bytes 6881284
  70.7 6.5 %copy-start.9 = (bf16[1,1792,1024]{2,1,0:T(8,128)(2,1)S(1)}, bf16[1,1792,1024]{2,1,0:T(8,128)(2,1)}, u32[]{:S(2)}) copy-start(bf16[1,1792,1024]{2,1,0:T(8,128)(2,1)} %param.12) | copy-start | bytes 11010052
  108.8 5.5 %copy-start.2 = (bf16[640,1792]{1,0:T(8,128)(2,1)}, bf16[640,1792]{1,0:T(8,128)(2,1)S(1)}, u32[]{:S(2)}) copy-start(bf16[640,1792]{1,0:T(8,128)(2,1)S(1)} %reshape.135) | copy-start | bytes 6881284
  108.8 5.5 %copy-start.6 = (bf16[640,1,1024]{2,0,1:T(8,128)(2,1)S(1)}, bf16[640,1,1024]{2,0,1:T(8,128)(2,1)}, u32[]{:S(2)}) copy-start(bf16[640,1,1024]{2,0,1:T(8,128)(2,1)} %fusion.31) | copy-start | bytes 3932164
  108.8 5.5 %copy-start.7 = (bf16[640,1,1024]{2,0,1:T(8,128)(2,1)S(1)}, bf16[640,1,1024]{2,0,1:T(8,128)(2,1)}, u32[]{:S(2)}) copy-start(bf16[640,1,1024]{2,0,1:T(8,128)(2,1)} %fusion.34) | copy-start | bytes 3932164
  116.5 75.1 %all-gather.3.cloned.1.call-start = ((), (), s32[]{:S(2)}) async-start(), calls=%async_computation.5 | async-start | bytes 1638400 | tf_op jit(solution)/shard_map/all_gather | solution.py:102
  160.4 57.4 %all-gather.5.cloned.1.call-start = ((), (), s32[]{:S(2)}) async-start(), calls=%async_computation.6 | async-start | bytes 1638400 | tf_op jit(solution)/shard_map/all_gather | solution.py:83
  161.6 10.9 %collective-permute-start = (bf16[160,1024]{1,0:T(8,128)(2,1)}, bf16[160,1024]{1,0:T(8,128)(2,1)S(1)}, u32[]{:S(2)}, u32[]{:S(2)}) collective-permute-start(bf16[160,1024]{1,0:T(8,128)(2,1)} %get-tuple-element.4), channel_id=1, source_target_pairs={{0,32},{32,64},{64,96},{96,0},{1,33},{33,65},{65,97},{97,1},{2,34}... | collective-permute-start | bytes 983048 | tf_op jit(solution)/shard_map/ppermute | solution.py:92
  161.9 12.6 %collective-permute-start.1 = (bf16[160,1024]{1,0:T(8,128)(2,1)}, bf16[160,1024]{1,0:T(8,128)(2,1)S(1)}, u32[]{:S(2)}, u32[]{:S(2)}) collective-permute-start(bf16[160,1024]{1,0:T(8,128)(2,1)} %get-tuple-element.4), channel_id=1, source_target_pairs={{0,96},{32,0},{64,32},{96,64},{1,97},{33,1},{65,33},{97,65},{2,98}... | collective-permute-start | bytes 983048 | tf_op jit(solution)/shard_map/ppermute | solution.py:97
  172.5 18.1 %collective-permute-start.2 = (bf16[160,1024]{1,0:T(8,128)(2,1)S(1)}, bf16[160,1024]{1,0:T(8,128)(2,1)S(1)}, u32[]{:S(2)}, u32[]{:S(2)}) collective-permute-start(bf16[160,1024]{1,0:T(8,128)(2,1)S(1)} %collective-permute-done), channel_id=1, source_target_pairs={{0,32},{32,64},{64,96},{96,0},{1,33},{33,65},{65,97},{97,1},{2,34}... | collective-permute-start | bytes 983048 | tf_op jit(solution)/shard_map/ppermute | solution.py:92
  190.7 1.1 copy-start.5
  191.7 5.2 %copy-start.10 = (bf16[1,1792,1024]{2,1,0:T(8,128)(2,1)S(1)}, bf16[1,1792,1024]{2,1,0:T(8,128)(2,1)}, u32[]{:S(2)}) copy-start(bf16[1,1792,1024]{2,1,0:T(8,128)(2,1)} %param.12) | copy-start | bytes 11010052
  203.1 14.7 %copy-start.3 = (bf16[640,1792]{1,0:T(8,128)(2,1)S(1)}, bf16[640,1792]{1,0:T(8,128)(2,1)}, u32[]{:S(2)}) copy-start(bf16[640,1792]{1,0:T(8,128)(2,1)} %copy-done.2) | copy-start | bytes 6881284
  203.1 45.0 %all-to-all-start.2 = ((bf16[32,20,1792]{2,1,0:T(8,128)(2,1)}), bf16[32,20,1792]{2,1,0:T(8,128)(2,1)}, u32[]{:S(2)}, u32[]{:S(2)}) async-start(bf16[32,20,1792]{2,1,0:T(8,128)(2,1)} %reshape.136), calls=%async_computation.3 | async-start | bytes 5505024 | tf_op jit(solution)/shard_map/all_to_all | solution.py:109
  248.1 8.8 %copy-start.1 = (bf16[512,1792]{1,0:T(8,128)(2,1)S(1)}, bf16[512,1792]{1,0:T(8,128)(2,1)}, u32[]{:S(2)}) copy-start(bf16[512,1792]{1,0:T(8,128)(2,1)} %param.8) | copy-start | bytes 5505028
Sparse Core Ops, SparseCore 0:
  116.6 41.2 reduce-scatter.1
  160.5 31.0 all-gather.2
  193.9 23.9 all-gather.4
